TPU v7x, 256 devices: a whole 4x4x8 slice. The times are simulated.
256 devices in a mesh: band: 32 (over x_lo, z, core), dom: 8 (over x_hi, y).
Axes of the slice: x: 4 (x_hi: 2, x_lo: 2; x = x_hi * 2 + x_lo), y: 4, z: 8, core: 2. Of those that a mesh axis runs over, the one named last changes fastest.
Arguments:
- states: float32 [64, 192, 64, 256], P('band', 'dom'), may hold values from -6 to 6
- potential: float32 [192, 64, 256], P('dom'), may hold values from 0 to 2
- rotation_panel: float32 [2, 64], P(None, 'band'), may hold values from -4 to 4
- owner: int32 [1], replicated, may hold values from 0 to 31
Outputs:
- rotated: float32 [64, 192, 64, 256], P('band', 'dom')
Inputs may be any that keep to these rules, and one draw needn't show every extreme that they name: owner is the index of one block of 2 states along the band axis.
All inputs are finite; a program needn't handle non-finite values.
Results may differ from a plain program's by a relative error of at most 0.00017.
Values sent between devices are 32-bit elements; how exact they have to be, the bound alone decides.
No kernel may reach another device: no remote copies, remote signals or barrier semaphores. Data moves between devices by JAX's collectives and lax.ppermute only.
A program may use at most 128 MiB of HBM per device.

v0:
```python
import jax
import jax.numpy as jnp
from jax import lax
from jax.sharding import PartitionSpec as P

DEG = 4
stencil_weights = (
    -5369.0 / 1800.0,
    12.0 / 7.0,
    -15.0 / 56.0,
    10.0 / 189.0,
    -1.0 / 112.0,
    2.0 / 1925.0,
    -1.0 / 16632.0,
)
center_value = 8.0
half_width = 5.0


def padded_2(shard, sides, width):
    for axis, dim in sides:
        size, length = (lax.axis_size(axis), shard.shape[dim])
        up = [(i, (i + 1) % size) for i in range(size - 1)]
        down = [(j, i) for i, j in up]
        last = lax.slice_in_dim(shard, length - width, length, axis=dim)
        initial = lax.slice_in_dim(shard, 0, width, axis=dim)
        before = lax.ppermute(last, axis, up)
        after = lax.ppermute(initial, axis, down)
        shard = jnp.concatenate([before, shard, after], axis=dim)
    return shard


def broadcast(block, axis, source):
    block = jnp.where(lax.axis_index(axis) == source, block, jnp.zeros_like(block))
    return lax.psum(block, axis)


def scaled_apply(padded, potential):
    length = potential.shape[0]
    middle = padded[:, 6 : 6 + length]
    along = 3.0 * stencil_weights[0] * middle
    for offset in range(1, 7):
        along = along + stencil_weights[offset] * (
            padded[:, 6 + offset : 6 + offset + length]
            + padded[:, 6 - offset : 6 - offset + length]
        )
    side = jnp.pad(middle, ((0, 0), (0, 0), (6, 6), (6, 6)))
    size_y = middle.shape[2]
    size_z = middle.shape[3]
    for offset in range(1, 7):
        pair_y = (
            side[:, :, 6 + offset : 6 + offset + size_y, 6 : 6 + size_z]
            + side[:, :, 6 - offset : 6 - offset + size_y, 6 : 6 + size_z]
        )
        pair_z = (
            side[:, :, 6 : 6 + size_y, 6 + offset : 6 + offset + size_z]
            + side[:, :, 6 : 6 + size_y, 6 - offset : 6 - offset + size_z]
        )
        along = along + stencil_weights[offset] * (pair_y + pair_z)
    applied = -0.5 * along + potential * middle
    return (applied - center_value * middle) / half_width


def face_rims(value):
    return padded_2(value, (("dom", 1),), 6)


def on_device(states, potential, rotation_panel, owner):
    previous = states
    current = scaled_apply(face_rims(states), potential)
    for step in range(DEG - 1):
        following = 2.0 * scaled_apply(face_rims(current), potential) - previous
        previous = current
        current = following
    panel = broadcast(current, "band", owner[0])
    mixed = jnp.einsum("sxyz,st->txyz", panel, rotation_panel, precision=lax.Precision.HIGHEST)
    return current + mixed


def solution(mesh):
    in_specs = (P("band", "dom", None, None), P("dom", None, None), P(None, "band"), P())
    out_specs = P("band", "dom", None, None)
    return jax.shard_map(
        on_device, mesh=mesh, in_specs=in_specs, out_specs=out_specs, check_vma=False
    )
```

profile of v0, /device:TPU:1, one launch (start us, length us, event | category | flops | bytes accessed | tf_op | source)
XLA Modules:
  0.0 736.0 jit_solution(4979216188630322081)
XLA Ops:
  6.5 4.4 copy.5
  11.5 4.3 collective-permute-start.1
  15.8 1.3 collective-permute-start
  17.1 14.7 %collective-permute-done.1 = f32[2,6,64,256]{3,0,2,1:T(2,128)S(1)} collective-permute-done((f32[2,6,64,256]{3,0,2,1:T(2,128)S(1)}, f32[2,6,64,256]{3,0,2,1:T(2,128)S(1)}, u32[]{:S(2)}, u32[]{:S(2)}) %collective-permute-start.1) | collective-permute-done | bytes 786464 | tf_op jit(solution)/shard_map/ppermute | solution.py:27
  33.0 6.0 constant_dynamic-update-slice_fusion.1
  40.1 73.3 %broadcast_multiply_fusion = (f32[2,24,64,256]{3,0,2,1:T(2,128)}, f32[2,24,64,256]{3,0,2,1:T(2,128)}) fusion(f32[2,24,64,256]{3,0,2,1:T(2,128)} %copy-done.3, f32[24,64,256]{2,1,0:T(8,128)S(1)} %copy-done.2, f32[2,30,64,256]{3,0,2,1:T(2,128)} %get-tuple-element.18, f32[2,30,64,256]{3,0,2,1:T(2,128)} %constant_dynamic-update-slice_fusion), kind=kLoop, calls=%fused_computation.291 | loop fusion | flops 43253760 | bytes 48758784 | tf_op jit(solution)/shard_map/div | solution.py:61
  113.4 1.9 fusion.150
  115.3 1.3 collective-permute-start.2
  116.6 5.0 collective-permute-start.3
  121.6 1.3 broadcast_multiply_fusion.1
  122.9 12.7 %collective-permute-done.2 = f32[2,6,64,256]{3,0,2,1:T(2,128)S(1)} collective-permute-done((f32[2,6,64,256]{3,0,2,1:T(2,128)S(1)}, f32[2,6,64,256]{3,0,2,1:T(2,128)S(1)}, u32[]{:S(2)}, u32[]{:S(2)}) %collective-permute-start.2) | collective-permute-done | bytes 786464 | tf_op jit(solution)/shard_map/ppermute | solution.py:28
  137.4 129.4 %multiply_subtract_fusion.2 = f32[2,24,64,256]{3,0,2,1:T(2,128)S(1)} fusion(f32[2,24,64,256]{3,0,2,1:T(2,128)} %get-tuple-element.8, f32[2,24,64,256]{3,0,2,1:T(2,128)} %get-tuple-element.7, f32[2,6,64,256]{3,0,2,1:T(2,128)} %copy-done.6, f32[2,6,64,256]{3,0,2,1:T(2,128)} %copy-done.5, f32[24,64,256]{2,1,0:T(8,128)} %broadcast_multiply_fusion.1, ...), kind=kLoop, calls=%fused_computation.288 | loop fusion | flops 53477376 | bytes 15728640 | tf_op jit(solution)/shard_map/sub | solution.py:72
  267.4 1.3 collective-permute-start.4
  268.7 5.6 collective-permute-start.5
  274.3 12.5 %collective-permute-done.4 = f32[2,6,64,256]{3,0,2,1:T(2,128)} collective-permute-done((f32[2,6,64,256]{3,0,2,1:T(2,128)S(1)}, f32[2,6,64,256]{3,0,2,1:T(2,128)}, u32[]{:S(2)}, u32[]{:S(2)}) %collective-permute-start.4) | collective-permute-done | bytes 786464 | tf_op jit(solution)/shard_map/ppermute | solution.py:28
  287.6 67.4 %multiply_subtract_fusion.1 = f32[2,24,64,256]{3,0,2,1:T(2,128)} fusion(f32[2,24,64,256]{3,0,2,1:T(2,128)S(1)} %multiply_subtract_fusion.2, f32[2,6,64,256]{3,0,2,1:T(2,128)} %collective-permute-done.5, f32[2,6,64,256]{3,0,2,1:T(2,128)} %collective-permute-done.4, f32[24,64,256]{2,1,0:T(8,128)} %param.5, f32[2,24,64,256]{3,0,2,1:T(2,128)} %get-tuple-element.8), kind=kLoop, calls=%fused_computation.287 | loop fusion | flops 54263808 | bytes 12582912 | tf_op jit(solution)/shard_map/sub | solution.py:72
  355.0 3.1 fusion.148
  358.1 1.3 collective-permute-start.6
  359.4 5.8 collective-permute-start.7
  365.8 11.1 %collective-permute-done.6 = f32[2,6,64,256]{3,0,2,1:T(2,128)} collective-permute-done((f32[2,6,64,256]{3,0,2,1:T(2,128)}, f32[2,6,64,256]{3,0,2,1:T(2,128)}, u32[]{:S(2)}, u32[]{:S(2)}) %collective-permute-start.6) | collective-permute-done | bytes 786464 | tf_op jit(solution)/shard_map/ppermute | solution.py:28
  377.8 84.9 %broadcast_select_fusion = (f32[2,24,64,256]{3,0,2,1:T(2,128)}, f32[2,24,64,256]{3,0,2,1:T(2,128)}) fusion(pred[]{:T(512)S(6)} %eq.3, f32[2,24,64,256]{3,0,2,1:T(2,128)S(1)} %multiply_subtract_fusion.2, f32[2,24,64,256]{3,0,2,1:T(2,128)} %multiply_subtract_fusion.1, f32[24,64,256]{2,1,0:T(8,128)} %param.5, f32[2,6,64,256]{3,0,2,1:T(2,128)} %collective-permute-done.7, ...), kind=kLoop, calls=%fused_computation.290 | loop fusion | flops 54263808 | bytes 15728641 | tf_op jit(solution)/shard_map/jit(_where)/select_n | solution.py:34
  462.8 251.0 %all-reduce.6.cloned.1.call-done = f32[2,24,64,256]{3,0,2,1:T(2,128)} async-done(((f32[2,24,64,256]{3,0,2,1:T(2,128)}), f32[2,24,64,256]{3,0,2,1:T(2,128)}) %all-reduce.6.cloned.1.call-update) | async-done | bytes 3145744 | tf_op jit(solution)/shard_map/psum | solution.py:35
  713.8 13.3 %bitcast_add_fusion = f32[2,24,64,256]{3,0,2,1:T(2,128)S(1)} fusion(f32[2,24,64,256]{3,0,2,1:T(2,128)S(1)} %copy-done.4, f32[2,24,64,256]{3,0,2,1:T(2,128)} %all-reduce.6.cloned.1.call-done, f32[2,2]{1,0:T(2,128)S(1)} %copy-done), kind=kOutput, calls=%fused_computation.285 | convolution fusion | flops 19660800 | bytes 9437200 | tf_op jit(solution)/shard_map/sxyz,st->txyz/dot_general | solution.py:76
  727.0 2.1 copy.15
  (24 shorter events, 7.0 us)
Async XLA Ops:
  6.5 707.2 %copy-start = (f32[2,2]{1,0:T(2,128)S(1)}, f32[2,2]{1,0:T(2,128)}, u32[]{:S(2)}) copy-start(f32[2,2]{1,0:T(2,128)} %param.6) | copy-start | bytes 52
  6.5 707.2 %all-reduce.6.cloned.1.call-start = ((), (), s32[]{:S(2)}) async-start(), calls=%async_computation | async-start | bytes 6291456 | tf_op jit(solution)/shard_map/psum | solution.py:35
  10.9 20.9 %copy-start.3 = (f32[2,24,64,256]{3,0,2,1:T(2,128)}, f32[2,24,64,256]{3,0,2,1:T(2,128)S(1)}, u32[]{:S(2)}) copy-start(f32[2,24,64,256]{3,0,2,1:T(2,128)S(1)} %copy.5) | copy-start | bytes 9437188
  10.9 22.1 %copy-start.1 = (f32[2,24,64,256]{3,2,1,0:T(8,128)S(1)}, f32[2,24,64,256]{3,2,1,0:T(8,128)}, u32[]{:S(2)}) copy-start(f32[2,24,64,256]{3,2,1,0:T(8,128)} %param.4) | copy-start | bytes 9437188
  11.5 20.3 %collective-permute-start.1 = (f32[2,6,64,256]{3,0,2,1:T(2,128)S(1)}, f32[2,6,64,256]{3,0,2,1:T(2,128)S(1)}, u32[]{:S(2)}, u32[]{:S(2)}) collective-permute-start(f32[2,6,64,256]{3,0,2,1:T(2,128)S(1)} %get-tuple-element.16), channel_id=1, source_target_pairs={{0,1},{1,2},{2,3},{3,4},{4,5},{5,6},{6,7},{8,9},{9,10},{10,11},{11... | collective-permute-start | bytes 2359304 | tf_op jit(solution)/shard_map/ppermute | solution.py:27
  15.8 23.1 %collective-permute-start = (f32[2,6,64,256]{3,0,2,1:T(2,128)S(1)}, f32[2,6,64,256]{3,0,2,1:T(2,128)S(1)}, u32[]{:S(2)}, u32[]{:S(2)}) collective-permute-start(f32[2,6,64,256]{3,0,2,1:T(2,128)S(1)} %get-tuple-element.15), channel_id=1, source_target_pairs={{1,0},{2,1},{3,2},{4,3},{5,4},{6,5},{7,6},{9,8},{10,9},{11,10},{12... | collective-permute-start | bytes 2359304 | tf_op jit(solution)/shard_map/ppermute | solution.py:28
  33.0 7.1 copy-start.2
  115.3 20.3 %collective-permute-start.2 = (f32[2,6,64,256]{3,0,2,1:T(2,128)S(1)}, f32[2,6,64,256]{3,0,2,1:T(2,128)S(1)}, u32[]{:S(2)}, u32[]{:S(2)}) collective-permute-start(f32[2,6,64,256]{3,0,2,1:T(2,128)S(1)} %get-tuple-element.13), channel_id=1, source_target_pairs={{1,0},{2,1},{3,2},{4,3},{5,4},{6,5},{7,6},{9,8},{10,9},{11,10},{12... | collective-permute-start | bytes 2359304 | tf_op jit(solution)/shard_map/ppermute | solution.py:28
  116.6 19.9 %collective-permute-start.3 = (f32[2,6,64,256]{3,0,2,1:T(2,128)S(1)}, f32[2,6,64,256]{3,0,2,1:T(2,128)S(1)}, u32[]{:S(2)}, u32[]{:S(2)}) collective-permute-start(f32[2,6,64,256]{3,0,2,1:T(2,128)S(1)} %get-tuple-element.14), channel_id=1, source_target_pairs={{0,1},{1,2},{2,3},{3,4},{4,5},{5,6},{6,7},{8,9},{9,10},{10,11},{11... | collective-permute-start | bytes 2359304 | tf_op jit(solution)/shard_map/ppermute | solution.py:27
  135.6 0.9 copy-start.5
  136.5 0.9 copy-start.6
  267.4 19.4 %collective-permute-start.4 = (f32[2,6,64,256]{3,0,2,1:T(2,128)S(1)}, f32[2,6,64,256]{3,0,2,1:T(2,128)}, u32[]{:S(2)}, u32[]{:S(2)}) collective-permute-start(f32[2,6,64,256]{3,0,2,1:T(2,128)S(1)} %get-tuple-element.11), channel_id=1, source_target_pairs={{1,0},{2,1},{3,2},{4,3},{5,4},{6,5},{7,6},{9,8},{10,9},{11,10},{12... | collective-permute-start | bytes 2359304 | tf_op jit(solution)/shard_map/ppermute | solution.py:28
  268.7 18.9 %collective-permute-start.5 = (f32[2,6,64,256]{3,0,2,1:T(2,128)S(1)}, f32[2,6,64,256]{3,0,2,1:T(2,128)}, u32[]{:S(2)}, u32[]{:S(2)}) collective-permute-start(f32[2,6,64,256]{3,0,2,1:T(2,128)S(1)} %get-tuple-element.12), channel_id=1, source_target_pairs={{0,1},{1,2},{2,3},{3,4},{4,5},{5,6},{6,7},{8,9},{9,10},{10,11},{11... | collective-permute-start | bytes 2359304 | tf_op jit(solution)/shard_map/ppermute | solution.py:27
  358.1 18.8 %collective-permute-start.6 = (f32[2,6,64,256]{3,0,2,1:T(2,128)}, f32[2,6,64,256]{3,0,2,1:T(2,128)}, u32[]{:S(2)}, u32[]{:S(2)}) collective-permute-start(f32[2,6,64,256]{3,0,2,1:T(2,128)} %get-tuple-element.9), channel_id=1, source_target_pairs={{1,0},{2,1},{3,2},{4,3},{5,4},{6,5},{7,6},{9,8},{10,9},{11,10},{12... | collective-permute-start | bytes 2359304 | tf_op jit(solution)/shard_map/ppermute | solution.py:28
  359.4 18.4 %collective-permute-start.7 = (f32[2,6,64,256]{3,0,2,1:T(2,128)}, f32[2,6,64,256]{3,0,2,1:T(2,128)}, u32[]{:S(2)}, u32[]{:S(2)}) collective-permute-start(f32[2,6,64,256]{3,0,2,1:T(2,128)} %get-tuple-element.10), channel_id=1, source_target_pairs={{0,1},{1,2},{2,3},{3,4},{4,5},{5,6},{6,7},{8,9},{9,10},{10,11},{11... | collective-permute-start | bytes 2359304 | tf_op jit(solution)/shard_map/ppermute | solution.py:27
  462.8 251.0 %copy-start.4 = (f32[2,24,64,256]{3,0,2,1:T(2,128)S(1)}, f32[2,24,64,256]{3,0,2,1:T(2,128)}, u32[]{:S(2)}) copy-start(f32[2,24,64,256]{3,0,2,1:T(2,128)} %get-tuple-element.6) | copy-start | bytes 9437188
Sparse Core Ops, SparseCore 0:
  462.9 250.7 all-reduce.5
where the time goes:
time: 736 us
  other arithmetic  356 us (48%)
  waiting for transfers between devices  305 us (41%)
  starting transfers between devices  25.8 us (4%)
  local copies, waits for them, and re-layouts  21.8 us (3%)
  between operations  14.2 us (2%)
  matrix products  13.3 us (2%)
    psum x1, waiting for transfers between devices, broadcast(): return lax.psum(block, axis)  251 us
    sub x2, other arithmetic, on_device(): following = 2.0 * scaled_apply(face_rims(current), potential) - previous  197 us
    select_n x1, other arithmetic, broadcast(): jnp.where(lax.axis_index(axis) == source, block, jnp.zeros_like(block))  84.9 us
    div x1, other arithmetic, scaled_apply(): return (applied - center_value * middle) / half_width  73.3 us
    ppermute x4, waiting for transfers between devices, padded_2(): after = lax.ppermute(initial, axis, down)  36.3 us
    ppermute x4, starting transfers between devices, padded_2(): before = lax.ppermute(last, axis, up)  20.7 us
    ppermute x4, waiting for transfers between devices, padded_2(): before = lax.ppermute(last, axis, up)  17.3 us
  transfers between devices with their start and end apart: 9, of which 8 were waited for; matrix products, arithmetic and copies ran while one was open for 1% of the time, Pallas kernels for 0%

commit v1 on v0

--- a/solution.py
+++ b/solution.py
@@ -32,7 +32,7 @@
 
 def broadcast(block, axis, source):
     block = jnp.where(lax.axis_index(axis) == source, block, jnp.zeros_like(block))
-    return lax.psum(block, axis)
+    return jnp.sum(lax.all_gather(block, axis), axis=0)
 
 
 def scaled_apply(padded, potential):

time: 736 us -> 1070 us (1.45)
  waiting for transfers between devices: 305 us -> 596 us
  other arithmetic: 356 us -> 389 us
    all_gather x0 -> x1, waiting for transfers between devices: none -> 542 us  [broadcast(): return jnp.sum(lax.all_gather(block, axis), axis=0)]
    psum x1 -> x0, waiting for transfers between devices: 251 us -> none  [broadcast(): return lax.psum(block, axis)]
    reduce_sum x0 -> x1, other arithmetic: none -> 30.8 us  [broadcast(): return jnp.sum(lax.all_gather(block, axis), axis=0)]
where the time goes in v1:
time: 1070 us
  waiting for transfers between devices  596 us (56%)
  other arithmetic  389 us (36%)
  local copies, waits for them, and re-layouts  27.5 us (3%)
  starting transfers between devices  25.7 us (2%)
  between operations  14.2 us (1%)
  matrix products  13.3 us (1%)
    all_gather x1, waiting for transfers between devices, broadcast(): return jnp.sum(lax.all_gather(block, axis), axis=0)  542 us
    sub x2, other arithmetic, on_device(): following = 2.0 * scaled_apply(face_rims(current), potential) - previous  197 us
    select_n x1, other arithmetic, broadcast(): jnp.where(lax.axis_index(axis) == source, block, jnp.zeros_like(block))  86.1 us
    div x1, other arithmetic, scaled_apply(): return (applied - center_value * middle) / half_width  74.3 us
    ppermute x4, waiting for transfers between devices, padded_2(): after = lax.ppermute(initial, axis, down)  36.8 us
    reduce_sum x1, other arithmetic, broadcast(): return jnp.sum(lax.all_gather(block, axis), axis=0)  30.8 us
  transfers between devices with their start and end apart: 9, of which 8 were waited for; matrix products, arithmetic and copies ran while one was open for 1% of the time, Pallas kernels for 0%

profile of v1, /device:TPU:1, one launch (start us, length us, event | category | flops | bytes accessed | tf_op | source)
XLA Modules:
  0.0 1065.8 jit_solution(14896020894821854795)
XLA Ops:
  6.5 4.4 copy.28
  10.9 1.7 copy-done.3
  13.1 4.2 collective-permute-start.1
  17.4 1.3 collective-permute-start
  18.7 14.8 %collective-permute-done.1 = f32[2,6,64,256]{3,0,2,1:T(2,128)S(1)} collective-permute-done((f32[2,6,64,256]{3,0,2,1:T(2,128)S(1)}, f32[2,6,64,256]{3,0,2,1:T(2,128)S(1)}, u32[]{:S(2)}, u32[]{:S(2)}) %collective-permute-start.1) | collective-permute-done | bytes 786464 | tf_op jit(solution)/shard_map/ppermute | solution.py:27
  34.7 5.9 constant_dynamic-update-slice_fusion.1
  41.8 74.3 %broadcast_multiply_fusion = (f32[2,24,64,256]{3,0,2,1:T(2,128)}, f32[2,24,64,256]{3,0,2,1:T(2,128)}) fusion(f32[2,24,64,256]{3,0,2,1:T(2,128)} %copy-done.3, f32[24,64,256]{2,1,0:T(8,128)} %param.5, f32[2,30,64,256]{3,0,2,1:T(2,128)} %get-tuple-element.18, f32[2,30,64,256]{3,0,2,1:T(2,128)} %constant_dynamic-update-slice_fusion), kind=kLoop, calls=%fused_computation.293 | loop fusion | flops 43253760 | bytes 48758784 | tf_op jit(solution)/shard_map/div | solution.py:61
  116.1 2.0 fusion.154
  119.4 5.0 collective-permute-start.3
  124.4 1.3 broadcast_multiply_fusion.1
  125.8 12.8 %collective-permute-done.2 = f32[2,6,64,256]{3,0,2,1:T(2,128)S(1)} collective-permute-done((f32[2,6,64,256]{3,0,2,1:T(2,128)S(1)}, f32[2,6,64,256]{3,0,2,1:T(2,128)S(1)}, u32[]{:S(2)}, u32[]{:S(2)}) %collective-permute-start.2) | collective-permute-done | bytes 786464 | tf_op jit(solution)/shard_map/ppermute | solution.py:28
  140.3 129.4 %multiply_subtract_fusion.2 = f32[2,24,64,256]{3,0,2,1:T(2,128)S(1)} fusion(f32[2,24,64,256]{3,0,2,1:T(2,128)} %get-tuple-element.8, f32[2,24,64,256]{3,0,2,1:T(2,128)} %get-tuple-element.7, f32[2,6,64,256]{3,0,2,1:T(2,128)} %copy-done.5, f32[2,6,64,256]{3,0,2,1:T(2,128)} %copy-done.4, f32[24,64,256]{2,1,0:T(8,128)} %broadcast_multiply_fusion.1, ...), kind=kLoop, calls=%fused_computation.288 | loop fusion | flops 53477376 | bytes 15728640 | tf_op jit(solution)/shard_map/sub | solution.py:72
  271.6 5.6 collective-permute-start.5
  277.2 12.7 %collective-permute-done.4 = f32[2,6,64,256]{3,0,2,1:T(2,128)} collective-permute-done((f32[2,6,64,256]{3,0,2,1:T(2,128)S(1)}, f32[2,6,64,256]{3,0,2,1:T(2,128)}, u32[]{:S(2)}, u32[]{:S(2)}) %collective-permute-start.4) | collective-permute-done | bytes 786464 | tf_op jit(solution)/shard_map/ppermute | solution.py:28
  290.7 67.4 %multiply_subtract_fusion.1 = f32[2,24,64,256]{3,0,2,1:T(2,128)} fusion(f32[2,24,64,256]{3,0,2,1:T(2,128)S(1)} %multiply_subtract_fusion.2, f32[2,6,64,256]{3,0,2,1:T(2,128)} %collective-permute-done.5, f32[2,6,64,256]{3,0,2,1:T(2,128)} %collective-permute-done.4, f32[24,64,256]{2,1,0:T(8,128)} %param.5, f32[2,24,64,256]{3,0,2,1:T(2,128)} %get-tuple-element.8), kind=kLoop, calls=%fused_computation.287 | loop fusion | flops 54263808 | bytes 12582912 | tf_op jit(solution)/shard_map/sub | solution.py:72
  358.1 3.1 fusion.152
  362.4 5.7 collective-permute-start.7
  368.8 11.3 %collective-permute-done.6 = f32[2,6,64,256]{3,0,2,1:T(2,128)} collective-permute-done((f32[2,6,64,256]{3,0,2,1:T(2,128)}, f32[2,6,64,256]{3,0,2,1:T(2,128)}, u32[]{:S(2)}, u32[]{:S(2)}) %collective-permute-start.6) | collective-permute-done | bytes 786464 | tf_op jit(solution)/shard_map/ppermute | solution.py:28
  381.0 86.1 %broadcast_select_fusion = (f32[2,24,64,256]{3,0,2,1:T(2,128)}, f32[2,24,64,256]{3,0,2,1:T(2,128)}) fusion(pred[]{:T(512)S(6)} %eq.3, f32[2,24,64,256]{3,0,2,1:T(2,128)S(1)} %multiply_subtract_fusion.2, f32[2,24,64,256]{3,0,2,1:T(2,128)} %multiply_subtract_fusion.1, f32[24,64,256]{2,1,0:T(8,128)} %param.5, f32[2,6,64,256]{3,0,2,1:T(2,128)} %collective-permute-done.7, ...), kind=kLoop, calls=%fused_computation.292 | loop fusion | flops 54263808 | bytes 15728641 | tf_op jit(solution)/shard_map/jit(_where)/select_n | solution.py:34
  467.1 4.0 copy.37
  471.2 541.6 %all-gather.3.cloned.1.call-done = f32[64,24,64,256]{3,2,1,0:T(8,128)} async-done(((f32[2,24,64,256]{3,2,1,0:T(8,128)}), f32[64,24,64,256]{3,2,1,0:T(8,128)}) %all-gather.3.cloned.1.call-update) | async-done | bytes 100663312 | tf_op jit(solution)/shard_map/all_gather | solution.py:35
  1012.7 30.8 %reduce_sum.9 = f32[2,24,64,256]{3,2,1,0:T(8,128)S(1)} reduce(f32[32,2,24,64,256]{4,3,2,1,0:T(8,128)} %bitcast.1, f32[]{:T(128)} %constant.35.clone.1), dimensions={0}, to_apply=%region_0.1 | reduce | flops 24379392 | bytes 103809024 | tf_op jit(solution)/shard_map/reduce_sum | solution.py:35
  1043.5 13.3 %bitcast_add_fusion = f32[2,24,64,256]{3,0,2,1:T(2,128)S(1)} fusion(f32[2,24,64,256]{3,0,2,1:T(2,128)} %get-tuple-element.6, f32[2,24,64,256]{3,2,1,0:T(8,128)S(1)} %reduce_sum.9, f32[2,2]{1,0:T(2,128)S(1)} %copy-done), kind=kOutput, calls=%fused_computation.285 | convolution fusion | flops 19660800 | bytes 9437200 | tf_op jit(solution)/shard_map/sxyz,st->txyz/dot_general | solution.py:76
  1056.8 2.1 copy.40
  (24 shorter events, 10.8 us)
Async XLA Ops:
  6.5 1037.0 %copy-start = (f32[2,2]{1,0:T(2,128)S(1)}, f32[2,2]{1,0:T(2,128)}, u32[]{:S(2)}) copy-start(f32[2,2]{1,0:T(2,128)} %param.6) | copy-start | bytes 52
  6.5 1006.2 %all-gather.3.cloned.1.call-start = ((), (), s32[]{:S(2)}) async-start(), calls=%async_computation | async-start | bytes 103809024 | tf_op jit(solution)/shard_map/all_gather | solution.py:35
  10.9 1.7 copy-start.3
  12.6 22.1 %copy-start.1 = (f32[2,24,64,256]{3,2,1,0:T(8,128)S(1)}, f32[2,24,64,256]{3,2,1,0:T(8,128)}, u32[]{:S(2)}) copy-start(f32[2,24,64,256]{3,2,1,0:T(8,128)} %param.4) | copy-start | bytes 9437188
  13.1 20.4 %collective-permute-start.1 = (f32[2,6,64,256]{3,0,2,1:T(2,128)S(1)}, f32[2,6,64,256]{3,0,2,1:T(2,128)S(1)}, u32[]{:S(2)}, u32[]{:S(2)}) collective-permute-start(f32[2,6,64,256]{3,0,2,1:T(2,128)S(1)} %get-tuple-element.16), channel_id=1, source_target_pairs={{0,1},{1,2},{2,3},{3,4},{4,5},{5,6},{6,7},{8,9},{9,10},{10,11},{11... | collective-permute-start | bytes 2359304 | tf_op jit(solution)/shard_map/ppermute | solution.py:27
  17.4 23.3 %collective-permute-start = (f32[2,6,64,256]{3,0,2,1:T(2,128)S(1)}, f32[2,6,64,256]{3,0,2,1:T(2,128)S(1)}, u32[]{:S(2)}, u32[]{:S(2)}) collective-permute-start(f32[2,6,64,256]{3,0,2,1:T(2,128)S(1)} %get-tuple-element.15), channel_id=1, source_target_pairs={{1,0},{2,1},{3,2},{4,3},{5,4},{6,5},{7,6},{9,8},{10,9},{11,10},{12... | collective-permute-start | bytes 2359304 | tf_op jit(solution)/shard_map/ppermute | solution.py:28
  116.1 8.3 copy-start.2
  118.1 20.4 %collective-permute-start.2 = (f32[2,6,64,256]{3,0,2,1:T(2,128)S(1)}, f32[2,6,64,256]{3,0,2,1:T(2,128)S(1)}, u32[]{:S(2)}, u32[]{:S(2)}) collective-permute-start(f32[2,6,64,256]{3,0,2,1:T(2,128)S(1)} %get-tuple-element.13), channel_id=1, source_target_pairs={{1,0},{2,1},{3,2},{4,3},{5,4},{6,5},{7,6},{9,8},{10,9},{11,10},{12... | collective-permute-start | bytes 2359304 | tf_op jit(solution)/shard_map/ppermute | solution.py:28
  119.4 20.0 %collective-permute-start.3 = (f32[2,6,64,256]{3,0,2,1:T(2,128)S(1)}, f32[2,6,64,256]{3,0,2,1:T(2,128)S(1)}, u32[]{:S(2)}, u32[]{:S(2)}) collective-permute-start(f32[2,6,64,256]{3,0,2,1:T(2,128)S(1)} %get-tuple-element.14), channel_id=1, source_target_pairs={{0,1},{1,2},{2,3},{3,4},{4,5},{5,6},{6,7},{8,9},{9,10},{10,11},{11... | collective-permute-start | bytes 2359304 | tf_op jit(solution)/shard_map/ppermute | solution.py:27
  138.5 0.9 copy-start.4
  139.5 0.9 copy-start.5
  270.3 19.6 %collective-permute-start.4 = (f32[2,6,64,256]{3,0,2,1:T(2,128)S(1)}, f32[2,6,64,256]{3,0,2,1:T(2,128)}, u32[]{:S(2)}, u32[]{:S(2)}) collective-permute-start(f32[2,6,64,256]{3,0,2,1:T(2,128)S(1)} %get-tuple-element.11), channel_id=1, source_target_pairs={{1,0},{2,1},{3,2},{4,3},{5,4},{6,5},{7,6},{9,8},{10,9},{11,10},{12... | collective-permute-start | bytes 2359304 | tf_op jit(solution)/shard_map/ppermute | solution.py:28
  271.6 19.1 %collective-permute-start.5 = (f32[2,6,64,256]{3,0,2,1:T(2,128)S(1)}, f32[2,6,64,256]{3,0,2,1:T(2,128)}, u32[]{:S(2)}, u32[]{:S(2)}) collective-permute-start(f32[2,6,64,256]{3,0,2,1:T(2,128)S(1)} %get-tuple-element.12), channel_id=1, source_target_pairs={{0,1},{1,2},{2,3},{3,4},{4,5},{5,6},{6,7},{8,9},{9,10},{10,11},{11... | collective-permute-start | bytes 2359304 | tf_op jit(solution)/shard_map/ppermute | solution.py:27
  361.2 19.0 %collective-permute-start.6 = (f32[2,6,64,256]{3,0,2,1:T(2,128)}, f32[2,6,64,256]{3,0,2,1:T(2,128)}, u32[]{:S(2)}, u32[]{:S(2)}) collective-permute-start(f32[2,6,64,256]{3,0,2,1:T(2,128)} %get-tuple-element.9), channel_id=1, source_target_pairs={{1,0},{2,1},{3,2},{4,3},{5,4},{6,5},{7,6},{9,8},{10,9},{11,10},{12... | collective-permute-start | bytes 2359304 | tf_op jit(solution)/shard_map/ppermute | solution.py:28
  362.4 18.6 %collective-permute-start.7 = (f32[2,6,64,256]{3,0,2,1:T(2,128)}, f32[2,6,64,256]{3,0,2,1:T(2,128)}, u32[]{:S(2)}, u32[]{:S(2)}) collective-permute-start(f32[2,6,64,256]{3,0,2,1:T(2,128)} %get-tuple-element.10), channel_id=1, source_target_pairs={{0,1},{1,2},{2,3},{3,4},{4,5},{5,6},{6,7},{8,9},{9,10},{10,11},{11... | collective-permute-start | bytes 2359304 | tf_op jit(solution)/shard_map/ppermute | solution.py:27
Sparse Core Ops, SparseCore 0:
  471.3 541.4 all-gather.2
